TPU v7x, 32 devices: a whole 2x2x4 slice. The times are simulated.
32 devices in a mesh: vx: 4 (over y, x), vy: 8 (over z, core).
Axes of the slice: x: 2, y: 2, z: 4, core: 2. Of those that a mesh axis runs over, the one named last changes fastest.
Arguments:
- hidden: bfloat16 [128, 5120], P(('vx', 'vy')), may hold values from -96 to 96
- unembed: bfloat16 [152064, 5120], P(('vx', 'vy')), may hold values from -2 to 2
- loss_mask: int32 [128], P(('vx', 'vy')), may hold values 0 or 1
- seq_ids: int32 [128], P(('vx', 'vy')), may hold values from 0 to 7, never falling along the last dimension, each value on 1 to 32 neighbouring positions
Outputs:
- entropy: float32 [128], P(('vx', 'vy'))
- seq_mean: float32 [8], replicated
Inputs may be any that keep to these rules, and one draw needn't show every extreme that they name: `seq_ids`: sequence numbers never fall along the tokens; each sequence has 1 to 32 tokens.
All inputs are finite; a program needn't handle non-finite values. No bound on the sum of `loss_mask` on one device may be relied on, other than what follows from the above.
Results may differ from a plain program's by a relative error of at most 0.0013.
Values may be sent and summed in bfloat16 or wider, within the bound.
A program may use at most 128 MiB of HBM per device.

v0:
```python
import jax
import jax.numpy as jnp
from jax import lax
from jax.sharding import PartitionSpec as P

SEQS = 8


def sequence_sums(entropy_rows, mask_rows, id_rows):
    member = (id_rows[:, None] == jnp.arange(SEQS, dtype=jnp.int32)[None, :]) & (
        mask_rows[:, None] > 0
    )
    partial_sums = jnp.sum(entropy_rows[:, None] * member.astype(jnp.float32), axis=0)
    partial_counts = jnp.sum(member.astype(jnp.int32), axis=0)
    return (partial_sums, partial_counts)


def per_device(hidden, unembed, loss_mask, seq_ids):
    tok_local = hidden.shape[0]
    all_mask, all_ids = (
        lax.all_gather(loss_mask, ("vx", "vy"), axis=0, tiled=True),
        lax.all_gather(seq_ids, ("vx", "vy"), axis=0, tiled=True),
    )
    logits = lax.dot_general(
        unembed,
        lax.all_gather(hidden, ("vx", "vy"), axis=0, tiled=True),
        (((1,), (1,)), ((), ())),
        preferred_element_type=jnp.float32,
    )
    peaked = jnp.max(logits, axis=0)
    shifted = logits - peaked[None, :]
    expval = jnp.exp(shifted)
    stats = jnp.stack([peaked, jnp.sum(expval, axis=0), jnp.sum(expval * shifted, axis=0)])
    peaked, totals, tilted = (stats[0], stats[1], stats[2])
    position = lax.axis_index(("vx", "vy")) * tok_local
    largest = lax.pmax(peaked, ("vx", "vy"))
    shift = peaked - largest
    factor = jnp.exp(shift)
    norms_all, tilts_all = lax.psum(
        (factor * totals, factor * (tilted + shift * totals)), ("vx", "vy")
    )
    entropy_all = jnp.log(norms_all) - tilts_all / norms_all
    entropy = lax.dynamic_slice_in_dim(entropy_all, position, tok_local)
    seq_sums, seq_counts = sequence_sums(entropy_all, all_mask, all_ids)
    seq_mean = seq_sums / jnp.maximum(seq_counts, 1).astype(jnp.float32)
    return (entropy, seq_mean)


def solution(mesh):
    in_specs = (P(("vx", "vy"), None), P(("vx", "vy"), None), P(("vx", "vy")), P(("vx", "vy")))
    out_specs = (P(("vx", "vy")), P())
    return jax.shard_map(
        per_device, mesh=mesh, in_specs=in_specs, out_specs=out_specs, check_vma=False
    )
```

profile of v0, /device:TPU:0, one launch (start us, length us, event | category | flops | bytes accessed | tf_op | source)
XLA Modules:
  0.0 179.5 jit_solution(8160077383454973072)
XLA Ops:
  7.2 0.0 all-gather.3.cloned.1.call-start
  7.2 0.7 all-gather.3.cloned.1.call-update
  7.9 0.9 dynamic-update-slice
  8.8 0.8 dynamic-update-slice.1
  9.6 42.0 %all-reduce.2 = (s32[128]{0:T(128)S(1)}, s32[128]{0:T(128)S(1)}) all-reduce(s32[128]{0:T(128)S(1)} %dynamic-update-slice, s32[128]{0:T(128)S(1)} %dynamic-update-slice.1), channel_id=1, replica_groups=mesh['vx'=4,'vy'=8] {'vx','vy'}, use_global_device_ids=true, to_apply=%add | all-reduce | flops 256 | bytes 2048
  51.6 0.1 convert_reduce_fusion
  51.7 16.3 %all-gather.3.cloned.1.call-done = bf16[32,4,5120]{2,1,0:T(4,128)(2,1)} async-done(((bf16[1,4,5120]{2,1,0:T(4,128)(2,1)}), bf16[32,4,5120]{2,1,0:T(4,128)(2,1)}) %all-gather.3.cloned.1.call-update) | async-done | bytes 1310736 | tf_op jit(solution)/shard_map/all_gather | solution.py:26
  68.0 3.3 %reshape.14 = bf16[128,5120]{1,0:T(8,128)(2,1)} reshape(bf16[32,4,5120]{2,1,0:T(4,128)(2,1)} %all-gather.3.cloned.1.call-done) | data formatting | bytes 2621440
  71.3 20.4 %fusion.2 = (f32[128]{0:T(128)S(1)}, f32[4752,128]{1,0:T(8,128)S(1)}) fusion(bf16[4752,5120]{1,0:T(8,128)(2,1)} %param.5, bf16[128,5120]{1,0:T(8,128)(2,1)} %reshape.14), kind=kOutput, calls=%fused_computation.12 | convolution fusion | flops 6229149696 | bytes 52404736 | tf_op jit(solution)/shard_map/dot_general | solution.py:24
  91.7 39.1 %pmax.7 = f32[128]{0:T(128)S(1)} all-reduce(f32[128]{0:T(128)S(1)} %get-tuple-element.10), channel_id=1, replica_groups=mesh['vx'=4,'vy'=8] {'vx','vy'}, use_global_device_ids=true, to_apply=%region_1.0 | all-reduce | flops 128 | bytes 1024 | tf_op jit(solution)/shard_map/pmax | solution.py:36
  130.9 0.7 exponential_reduce_fusion
  131.5 39.9 %all-reduce.3 = (f32[128]{0:T(128)S(1)}, f32[128]{0:T(128)S(1)}) all-reduce(f32[128]{0:T(128)S(1)} %get-tuple-element.9, f32[128]{0:T(128)S(1)} %get-tuple-element.8), channel_id=1, replica_groups=mesh['vx'=4,'vy'=8] {'vx','vy'}, use_global_device_ids=true, to_apply=%region_5.0 | all-reduce | flops 256 | bytes 2048 | tf_op jit(solution)/shard_map/psum | solution.py:39
  171.5 0.1 select_reduce_fusion
  171.6 0.6 dynamic_slice.3
  172.2 0.5 convert_divide_fusion
  (5 shorter events, 0.0 us)
Async XLA Ops:
  7.2 60.9 %all-gather.3.cloned.1.call-start = ((), (), s32[]{:S(2)}) async-start(), calls=%async_computation | async-start | bytes 1351680 | tf_op jit(solution)/shard_map/all_gather | solution.py:26
Sparse Core Ops, SparseCore 0:
  10.8 57.1 all-gather.2
where the time goes:
time: 180 us
  blocking collectives  121 us (67%)
  matrix products  20.4 us (11%)
  waiting for transfers between devices  17 us (9%)
  between operations  14.1 us (8%)
  local copies, waits for them, and re-layouts  5.59 us (3%)
    unnamed x1, blocking collectives  42 us
    psum x1, blocking collectives, per_device(): lax.psum((factor * totals, factor * (tilted + shift * totals)), ('vx', 'v...  39.9 us
    pmax x1, blocking collectives, per_device(): largest = lax.pmax(peaked, ('vx', 'vy'))  39.1 us
    dot_general x1, matrix products, per_device(): lax.dot_general(unembed, lax.all_gather(hidden, ('vx', 'vy'), axis=0, til...  20.4 us
    all_gather x1, waiting for transfers between devices, per_device(): lax.all_gather(hidden, ('vx', 'vy'), axis=0, tiled=True)  16.3 us
    unnamed x5, local copies, waits for them, and re-layouts  5 us
  transfers between devices with their start and end apart: 1, of which 1 were waited for; matrix products, arithmetic and copies ran while one was open for 1% of the time, Pallas kernels for 0%

commit v1 on v0

v1 whole, which is shorter than its diff:
```python
import functools

import jax
import jax.numpy as jnp
from jax import lax
from jax.experimental import pallas as pl
from jax.experimental.pallas import tpu as pltpu
from jax.sharding import PartitionSpec as P

SEQS = 8
CORES = 2
MESH = pl.DeviceIdType.MESH
F32 = jnp.float32


def rows_per_chunk(rows, most=512):
    fits = [c for c in range(16, most + 1, 16) if rows % c == 0]
    return max(fits) if fits else rows


def kernel(
    nx, ny, chunk,
    hidden, unembed, mask, ids,
    entropy, seq_mean,
    weights, blocks, tokens_t, stats, stats_all,
    w_sem, send_sem, recv_sem, own_sem, stat_send, stat_recv,
):
    n, nz = nx * ny, ny // CORES
    tok, depth = hidden.shape
    total = n * tok
    chunks = unembed.shape[0] // chunk
    vx, vy = lax.axis_index("vx"), lax.axis_index("vy")
    z, core = vy // CORES, vy % CORES
    me = vx * ny + vy

    def w_copy(i):
        rows = pl.ds(i * chunk, chunk)
        return pltpu.make_async_copy(unembed.at[rows], weights.at[rows], w_sem.at[i])

    own = pltpu.make_async_copy(hidden, blocks.at[me], own_sem)
    own.start()
    for i in range(chunks):
        w_copy(i).start()

    barrier = pltpu.get_barrier_semaphore()
    for d in range(1, nx):
        pl.semaphore_signal(barrier, inc=1, device_id=((vx + d) % nx, vy), device_id_type=MESH)
    for d in range(1, nz):
        pl.semaphore_signal(
            barrier, inc=1, device_id=(vx, ((z + d) % nz) * CORES + core), device_id_type=MESH
        )
    pl.semaphore_signal(barrier, inc=1, device_id=(vx, z * CORES + 1 - core), device_id_type=MESH)
    pl.semaphore_wait(barrier, nx + nz - 1)

    def send(source, slot, x, y):
        pltpu.make_async_remote_copy(
            src_ref=source, dst_ref=blocks.at[slot], send_sem=send_sem,
            recv_sem=recv_sem.at[slot], device_id=(x, y), device_id_type=MESH,
        ).start()

    def arrived(slot):
        pltpu.make_async_remote_copy(
            src_ref=blocks.at[slot], dst_ref=blocks.at[slot], send_sem=send_sem,
            recv_sem=recv_sem.at[slot], device_id=(vx, vy), device_id_type=MESH,
        ).wait_recv()

    far = sorted(range(1, nz), key=lambda d: min(d, nz - d))

    def along_z(source, slot):
        for d in far:
            send(source, slot, vx, ((z + d) % nz) * CORES + core)

    def to_partner(source, slot):
        send(source, slot, vx, z * CORES + 1 - core)

    for d in range(1, nx):
        send(hidden, me, (vx + d) % nx, vy)
    along_z(hidden, me)
    to_partner(hidden, me)
    for d in range(1, nx):
        slot = ((vx + d) % nx) * ny + vy
        arrived(slot)
        along_z(blocks.at[slot], slot)
        to_partner(blocks.at[slot], slot)
    for e in range(nx):
        for d in far:
            slot = ((vx + e) % nx) * ny + ((z + d) % nz) * CORES + core
            arrived(slot)
            to_partner(blocks.at[slot], slot)
    for e in range(nx):
        for d in range(nz):
            arrived(((vx + e) % nx) * ny + ((z + d) % nz) * CORES + 1 - core)
    own.wait()

    width = 512 if depth % 512 == 0 else depth

    @pl.loop(0, depth // width)
    def _(i):
        cols = pl.ds(pl.multiple_of(i * width, width), width)
        tokens_t[cols, :] = blocks[:, :, cols].reshape(total, width).T

    def step(i, carry):
        peak, norm, tilt = carry
        rows = pl.ds(pl.multiple_of(i * chunk, chunk), chunk)
        w_copy(i).wait()
        logits = jnp.dot(weights[rows, :], tokens_t[...], preferred_element_type=F32)
        top = jnp.maximum(peak, jnp.max(logits, axis=0, keepdims=True))
        shifted = logits - top
        value = jnp.exp(shifted)
        shift = peak - top
        factor = jnp.exp(shift)
        return (
            top,
            factor * norm + jnp.sum(value, axis=0, keepdims=True),
            factor * (tilt + shift * norm) + jnp.sum(value * shifted, axis=0, keepdims=True),
        )

    low = jnp.full((1, total), jnp.finfo(jnp.float32).min / 4, F32)
    zero = jnp.zeros((1, total), F32)
    peak, norm, tilt = lax.fori_loop(0, chunks, step, (low, zero, zero))

    lane = lax.broadcasted_iota(jnp.int32, (1, total), 1)
    code = jnp.zeros((1, total), jnp.int32)
    for j in range(tok):
        mine = jnp.where(mask[j] > 0, ids[j] + 1, 0)
        code = jnp.where(lane == me * tok + j, mine, code)
    stats[0:1, :] = peak
    stats[1:2, :] = norm
    stats[2:3, :] = tilt
    stats[3:4, :] = code.astype(F32)

    def stat_copy(d):
        peer = (me + d) % n
        return pltpu.make_async_remote_copy(
            src_ref=stats, dst_ref=stats_all.at[me], send_sem=stat_send, recv_sem=stat_recv,
            device_id=(peer // ny, peer % ny), device_id_type=MESH,
        )

    @pl.loop(1, n)
    def _(d):
        stat_copy(d).start()

    stats_all[me] = stats[...]
    everyone = pltpu.make_async_remote_copy(
        src_ref=stats_all.at[pl.ds(0, n - 1)], dst_ref=stats_all.at[pl.ds(0, n - 1)],
        send_sem=stat_send, recv_sem=stat_recv, device_id=(vx, vy), device_id_type=MESH,
    )
    everyone.wait_recv()

    peaks, norms, tilts = stats_all[:, 0, :], stats_all[:, 1, :], stats_all[:, 2, :]
    codes = jnp.sum(stats_all[:, 3, :], axis=0, keepdims=True)
    shift = peaks - jnp.max(peaks, axis=0, keepdims=True)
    factor = jnp.exp(shift)
    norm = jnp.sum(factor * norms, axis=0, keepdims=True)
    tilt = jnp.sum(factor * (tilts + shift * norms), axis=0, keepdims=True)
    value = jnp.log(norm) - tilt / norm

    slot = lax.broadcasted_iota(jnp.int32, (1, tok), 1)
    out = jnp.zeros((1, tok), F32)
    for j in range(tok):
        one = jnp.sum(jnp.where(lane == me * tok + j, value, 0.0), axis=1, keepdims=True)
        out = jnp.where(slot == j, one, out)
    entropy[...] = out
    seq = lax.broadcasted_iota(jnp.int32, (SEQS, total), 0)
    member = (jnp.broadcast_to(codes, (SEQS, total)) == (seq + 1).astype(F32)).astype(F32)
    sums = jnp.sum(member * jnp.broadcast_to(value, (SEQS, total)), axis=1, keepdims=True)
    counts = jnp.sum(member, axis=1, keepdims=True)
    mean = sums / jnp.maximum(counts, 1.0)
    diag = lax.broadcasted_iota(jnp.int32, (SEQS, SEQS), 0) == lax.broadcasted_iota(
        jnp.int32, (SEQS, SEQS), 1
    )
    seq_mean[...] = jnp.sum(jnp.where(diag, mean, 0.0), axis=0, keepdims=True)

    everyone.wait_send()
    pltpu.make_async_remote_copy(
        src_ref=blocks.at[pl.ds(0, n - 1)], dst_ref=blocks.at[pl.ds(0, n - 1)],
        send_sem=send_sem, recv_sem=own_sem, device_id=(vx, vy), device_id_type=MESH,
    ).wait_send()


def solution(mesh):
    nx, ny = mesh.shape["vx"], mesh.shape["vy"]
    n = nx * ny

    def per_device(hidden, unembed, loss_mask, seq_ids):
        tok, depth = hidden.shape
        rows, total = unembed.shape[0], tok * n
        chunk = rows_per_chunk(rows)
        entropy, seq_mean = pl.pallas_call(
            functools.partial(kernel, nx, ny, chunk),
            out_shape=[
                jax.ShapeDtypeStruct((1, tok), F32),
                jax.ShapeDtypeStruct((1, SEQS), F32),
            ],
            in_specs=[pl.BlockSpec(memory_space=pl.ANY)] * 2
            + [pl.BlockSpec(memory_space=pltpu.SMEM)] * 2,
            out_specs=[pl.BlockSpec(memory_space=pltpu.VMEM)] * 2,
            scratch_shapes=[
                pltpu.VMEM((rows, depth), jnp.bfloat16),
                pltpu.VMEM((n, tok, depth), jnp.bfloat16),
                pltpu.VMEM((depth, total), jnp.bfloat16),
                pltpu.VMEM((8, total), F32),
                pltpu.VMEM((n, 8, total), F32),
                pltpu.SemaphoreType.DMA((rows // chunk,)),
                pltpu.SemaphoreType.DMA,
                pltpu.SemaphoreType.DMA((n,)),
                pltpu.SemaphoreType.DMA,
                pltpu.SemaphoreType.DMA,
                pltpu.SemaphoreType.DMA,
            ],
            compiler_params=pltpu.CompilerParams(
                collective_id=0, has_side_effects=True, vmem_limit_bytes=62 * 1024 * 1024
            ),
        )(hidden, unembed, loss_mask, seq_ids)
        return entropy.reshape(tok), seq_mean.reshape(SEQS)

    in_specs = (P(("vx", "vy"), None), P(("vx", "vy"), None), P(("vx", "vy")), P(("vx", "vy")))
    return jax.shard_map(
        per_device, mesh=mesh, in_specs=in_specs, out_specs=(P(("vx", "vy")), P()), check_vma=False
    )
```

time: 180 us -> 48.4 us (0.27)
  blocking collectives: 121 us -> 0 us
  Pallas kernels: 0 us -> 45.3 us
  matrix products: 20.4 us -> 0 us
  waiting for transfers between devices: 17 us -> 0 us
  between operations: 14.1 us -> 0.64 us
  local copies, waits for them, and re-layouts: 5.59 us -> 2.25 us
    pallas_call x0 -> x1, Pallas kernels: none -> 45.3 us  [per_device(): pl.pallas_call(functools.partial(kernel, nx, ny, chunk), out_shape=[jax.S...]
    unnamed x1 -> x0, blocking collectives: 42 us -> none
    psum x1 -> x0, blocking collectives: 39.9 us -> none  [per_device(): lax.psum((factor * totals, factor * (tilted + shift * totals)), ('vx', 'v...]
    pmax x1 -> x0, blocking collectives: 39.1 us -> none  [per_device(): largest = lax.pmax(peaked, ('vx', 'vy'))]
    dot_general x1 -> x0, matrix products: 20.4 us -> none  [per_device(): lax.dot_general(unembed, lax.all_gather(hidden, ('vx', 'vy'), axis=0, til...]
    all_gather x1 -> x0, waiting for transfers between devices: 16.3 us -> none  [per_device(): lax.all_gather(hidden, ('vx', 'vy'), axis=0, tiled=True)]
    unnamed x5 -> x2, local copies, waits for them, and re-layouts: 5 us -> 2.25 us
  transfers between devices with their start and end apart: 1 -> 0, of which waited for: 1 -> 0; matrix products, arithmetic and copies ran while one was open for 1% -> 0% of each run, Pallas kernels for 0% -> 0%
where the time goes in v1:
time: 48.4 us; the launch traced here: 48.2 us
  Pallas kernels  45.3 us (94%)
  local copies, waits for them, and re-layouts  2.25 us (5%)
  between operations  0.64 us (1%)
    pallas_call x1, Pallas kernels, per_device(): pl.pallas_call(functools.partial(kernel, nx, ny, chunk), out_shape=[jax.S...  45.3 us
    unnamed x2, local copies, waits for them, and re-layouts  2.25 us

profile of v1, /device:TPU:0, one launch (start us, length us, event | category | flops | bytes accessed | tf_op | source)
XLA Modules:
  0.0 48.2 jit_solution(17148538477404357391)
XLA Ops:
  0.6 45.3 %shard_map.59 = (f32[1,4]{1,0:T(1,128)}, f32[1,8]{1,0:T(1,128)}) custom-call(bf16[4,5120]{1,0:T(4,128)(2,1)} %hidden.1, bf16[4752,5120]{1,0:T(8,128)(2,1)} %unembed.1, s32[4]{0:T(128)} %mask.1, s32[4]{0:T(128)} %ids.1), custom_call_target="tpu_custom_call" | custom-call | tf_op jit(solution)/shard_map/pallas_call | solution.py:189
  46.0 1.1 %copy.8 = f32[4]{0:T(128)} copy(f32[4]{0:T(128)} %bitcast.3) | data formatting | bytes 32
  47.1 1.1 %copy.9 = f32[8]{0:T(128)} copy(f32[8]{0:T(128)} %bitcast.2) | data formatting | bytes 64

commit v2 on v1

--- a/solution.py
+++ b/solution.py
@@ -73,18 +73,19 @@
     def to_partner(source, slot):
         send(source, slot, vx, z * CORES + 1 - core)
 
+    along_z(hidden, me)
     for d in range(1, nx):
         send(hidden, me, (vx + d) % nx, vy)
-    along_z(hidden, me)
     to_partner(hidden, me)
-    for d in range(1, nx):
-        slot = ((vx + d) % nx) * ny + vy
+    for e in far:
+        slot = vx * ny + ((z + e) % nz) * CORES + core
         arrived(slot)
-        along_z(blocks.at[slot], slot)
+        for d in range(1, nx):
+            send(blocks.at[slot], slot, (vx + d) % nx, vy)
         to_partner(blocks.at[slot], slot)
-    for e in range(nx):
-        for d in far:
-            slot = ((vx + e) % nx) * ny + ((z + d) % nz) * CORES + core
+    for e in [0] + far:
+        for d in range(1, nx):
+            slot = ((vx + d) % nx) * ny + ((z + e) % nz) * CORES + core
             arrived(slot)
             to_partner(blocks.at[slot], slot)
     for e in range(nx):
@@ -192,15 +193,15 @@
                 jax.ShapeDtypeStruct((1, tok), F32),
                 jax.ShapeDtypeStruct((1, SEQS), F32),
             ],
-            in_specs=[pl.BlockSpec(memory_space=pl.ANY)] * 2
+            in_specs=[pl.BlockSpec(memory_space=pltpu.VMEM), pl.BlockSpec(memory_space=pl.ANY)]
             + [pl.BlockSpec(memory_space=pltpu.SMEM)] * 2,
             out_specs=[pl.BlockSpec(memory_space=pltpu.VMEM)] * 2,
             scratch_shapes=[
                 pltpu.VMEM((rows, depth), jnp.bfloat16),
                 pltpu.VMEM((n, tok, depth), jnp.bfloat16),
                 pltpu.VMEM((depth, total), jnp.bfloat16),
-                pltpu.VMEM((8, total), F32),
-                pltpu.VMEM((n, 8, total), F32),
+                pltpu.VMEM((4, total), F32),
+                pltpu.VMEM((n, 4, total), F32),
                 pltpu.SemaphoreType.DMA((rows // chunk,)),
                 pltpu.SemaphoreType.DMA,
                 pltpu.SemaphoreType.DMA((n,)),

time: 48.4 us -> 42.7 us (0.88)
  Pallas kernels: 45.3 us -> 39.6 us
    pallas_call x1, Pallas kernels: 45.3 us -> 39.6 us  [per_device(): pl.pallas_call(functools.partial(kernel, nx, ny, chunk), out_shape=[jax.S...]
where the time goes in v2:
time: 42.7 us; the launch traced here: 42.5 us
  Pallas kernels  39.6 us (93%)
  local copies, waits for them, and re-layouts  2.25 us (5%)
  between operations  0.64 us (1%)
    pallas_call x1, Pallas kernels, per_device(): pl.pallas_call(functools.partial(kernel, nx, ny, chunk), out_shape=[jax.S...  39.6 us
    unnamed x2, local copies, waits for them, and re-layouts  2.25 us

profile of v2, /device:TPU:0, one launch (start us, length us, event | category | flops | bytes accessed | tf_op | source)
XLA Modules:
  0.0 42.5 jit_solution(8367357814169664916)
XLA Ops:
  0.6 39.6 %shard_map.59 = (f32[1,4]{1,0:T(1,128)}, f32[1,8]{1,0:T(1,128)}) custom-call(bf16[4,5120]{1,0:T(4,128)(2,1)} %hidden.1, bf16[4752,5120]{1,0:T(8,128)(2,1)} %unembed.1, s32[4]{0:T(128)} %mask.1, s32[4]{0:T(128)} %ids.1), custom_call_target="tpu_custom_call" | custom-call | tf_op jit(solution)/shard_map/pallas_call | solution.py:190
  40.2 1.1 %copy.8 = f32[4]{0:T(128)} copy(f32[4]{0:T(128)} %bitcast.3) | data formatting | bytes 32
  41.3 1.1 %copy.9 = f32[8]{0:T(128)} copy(f32[8]{0:T(128)} %bitcast.2) | data formatting | bytes 64
